TPU v7x, 32 devices: a whole 2x2x4 slice. The times are simulated.
32 devices in a mesh: dp: 8 (over z, core), seq: 4 (over y, x).
Axes of the slice: x: 2, y: 2, z: 4, core: 2. Of those that a mesh axis runs over, the one named last changes fastest.
Arguments:
- enc_final: bfloat16 [8, 96, 4096], P('dp', 'seq'), may hold values from -6 to 6
- norm_gain: float32 [4096], replicated, may hold values from 0.1 to 1.9
- dec_queries: bfloat16 [2, 8, 512, 2048], P(None, 'dp', 'seq'), may hold values from -48 to 48
- out_grad: bfloat16 [2, 8, 512, 2048], P(None, 'dp', 'seq'), may hold values from -6 to 6
- enc_keys: bfloat16 [2, 8, 96, 2048], P(None, 'dp', 'seq'), may hold values from -6 to 6
- enc_values: bfloat16 [2, 8, 96, 2048], P(None, 'dp', 'seq'), may hold values from -6 to 6
- key_weight: bfloat16 [2, 4096, 2048], P(None, None, 'seq'), may hold values from -0.09375 to 0.09375
- value_weight: bfloat16 [2, 4096, 2048], P(None, None, 'seq'), may hold values from -0.09375 to 0.09375
Outputs:
- enc_grad: bfloat16 [8, 96, 4096], P('dp', 'seq')
- gain_grad: float32 [4096], replicated
All inputs are finite; a program needn't handle non-finite values.
Results may differ from a plain program's by a relative error of at most 0.007.
Values may be sent and summed in bfloat16 or wider, within the bound.
No kernel may reach another device: no remote copies, remote signals or barrier semaphores. Data moves between devices by JAX's collectives and lax.ppermute only.
A program may use at most 128 MiB of HBM per device.

v0:
```python
import jax
import jax.numpy as jnp
from jax import lax
from jax.sharding import PartitionSpec as P

HEAD_DIM = 64


def head_grads(query_rows, grad_rows, key_rows, value_rows, head_size):
    dec_count = query_rows.shape[0]
    enc_count = key_rows.shape[0]
    head_count = query_rows.shape[1] // head_size
    query_heads = query_rows.reshape(dec_count, head_count, head_size)
    grad_heads = grad_rows.reshape(dec_count, head_count, head_size)
    key_heads = key_rows.reshape(enc_count, head_count, head_size)
    value_heads = value_rows.reshape(enc_count, head_count, head_size)
    scores = jnp.einsum("qhd,khd->hqk", query_heads, key_heads, preferred_element_type=jnp.float32)
    row_peak = jnp.max(scores, axis=-1, keepdims=True)
    shifted = jnp.exp(scores - row_peak)
    weights = shifted / jnp.sum(shifted, axis=-1, keepdims=True)
    prob_grad = jnp.einsum(
        "qhd,khd->hqk", grad_heads, value_heads, preferred_element_type=jnp.float32
    )
    row_delta = jnp.sum(weights * prob_grad, axis=-1, keepdims=True)
    score_grad = (weights * (prob_grad - row_delta)).astype(jnp.bfloat16)
    value_grad = jnp.einsum(
        "hqk,qhd->khd", weights.astype(jnp.bfloat16), grad_heads, preferred_element_type=jnp.float32
    )
    key_grad = jnp.einsum(
        "hqk,qhd->khd", score_grad, query_heads, preferred_element_type=jnp.float32
    )
    return (key_grad.reshape(enc_count, -1), value_grad.reshape(enc_count, -1))


def body(
    enc_final, norm_gain, dec_queries, out_grad, enc_keys, enc_values, key_weight, value_weight
):
    layer_count = dec_queries.shape[0]
    head_size = HEAD_DIM
    key_parts = []
    value_parts = []
    for layer_index in range(layer_count):
        query_rows = dec_queries[layer_index, 0]
        grad_rows = out_grad[layer_index, 0]
        key_rows = enc_keys[layer_index, 0]
        value_rows = enc_values[layer_index, 0]
        query_cols, grad_cols, key_cols, value_cols = (
            lax.all_to_all(query_rows, "seq", split_axis=1, concat_axis=0, tiled=True),
            lax.all_to_all(grad_rows, "seq", split_axis=1, concat_axis=0, tiled=True),
            lax.all_to_all(key_rows, "seq", split_axis=1, concat_axis=0, tiled=True),
            lax.all_to_all(value_rows, "seq", split_axis=1, concat_axis=0, tiled=True),
        )
        key_sum, value_sum = head_grads(query_cols, grad_cols, key_cols, value_cols, head_size)
        key_parts.append(key_sum.astype(jnp.bfloat16))
        value_parts.append(value_sum.astype(jnp.bfloat16))
    model_width = enc_final.shape[2]
    running = jnp.zeros((lax.axis_size("seq") * enc_final.shape[1], model_width), jnp.float32)
    for layer_index in range(layer_count):
        key_slice = key_parts[layer_index]
        value_slice = value_parts[layer_index]
        running = running + jnp.einsum(
            "rc,dc->rd", key_slice, key_weight[layer_index], preferred_element_type=jnp.float32
        )
        running = running + jnp.einsum(
            "rc,dc->rd", value_slice, value_weight[layer_index], preferred_element_type=jnp.float32
        )
    state_grad = lax.psum_scatter(running, "seq", scatter_dimension=0, tiled=True)
    final_float = enc_final[0].astype(jnp.float32)
    inv_rms = lax.rsqrt(jnp.mean(final_float * final_float, axis=-1, keepdims=True) + 1e-06)
    normed = final_float * inv_rms
    scaled = norm_gain[None, :] * state_grad
    grad_rows_out = inv_rms * (scaled - normed * jnp.mean(scaled * normed, axis=-1, keepdims=True))
    gain_term = jnp.sum(state_grad * normed, axis=0)
    gain_piece = lax.psum_scatter(gain_term, "seq", scatter_dimension=0, tiled=True)
    gain_piece = lax.psum(gain_piece, "dp")
    gain_total = lax.all_gather(gain_piece, "seq", axis=0, tiled=True)
    gain_grad = gain_total / lax.axis_size("dp")
    return (grad_rows_out.astype(jnp.bfloat16)[None], gain_grad)


def solution(mesh):
    placed = (
        P("dp", "seq", None),
        P(),
        P(None, "dp", "seq", None),
        P(None, "dp", "seq", None),
        P(None, "dp", "seq", None),
        P(None, "dp", "seq", None),
        P(None, None, "seq"),
        P(None, None, "seq"),
    )
    return jax.shard_map(
        body, mesh=mesh, in_specs=placed, out_specs=(P("dp", "seq", None), P()), check_vma=False
    )
```

profile of v0, /device:TPU:0, one launch (start us, length us, event | category | flops | bytes accessed | tf_op | source)
XLA Modules:
  0.0 180.6 jit_solution(3794831154180647183)
XLA Ops:
  7.2 1.0 fusion.43
  8.9 5.2 %all-to-all-start.1 = ((bf16[24,4,512]{2,0,1:T(8,128)(2,1)}), bf16[24,4,512]{2,0,1:T(8,128)(2,1)S(1)}, u32[]{:S(2)}, u32[]{:S(2)}) async-start(bf16[24,4,512]{2,0,1:T(8,128)(2,1)} %copy.32), calls=%async_computation.1 | async-start | bytes 196608 | tf_op jit(solution)/shard_map/all_to_all | solution.py:50
  15.8 3.3 %all-to-all-done.1 = bf16[24,4,512]{2,0,1:T(8,128)(2,1)S(1)} async-done(((bf16[24,4,512]{2,0,1:T(8,128)(2,1)}), bf16[24,4,512]{2,0,1:T(8,128)(2,1)S(1)}, u32[]{:S(2)}, u32[]{:S(2)}) %all-to-all-start.1) | async-done | bytes 98336 | tf_op jit(solution)/shard_map/all_to_all | solution.py:50
  19.1 3.3 %all-to-all-start.3 = ((bf16[24,4,512]{2,0,1:T(8,128)(2,1)}), bf16[24,4,512]{2,0,1:T(8,128)(2,1)S(1)}, u32[]{:S(2)}, u32[]{:S(2)}) async-start(bf16[24,4,512]{2,0,1:T(8,128)(2,1)} %copy.36), calls=%async_computation.3 | async-start | bytes 196608 | tf_op jit(solution)/shard_map/all_to_all | solution.py:51
  23.1 4.2 %all-to-all-done.3 = bf16[24,4,512]{2,0,1:T(8,128)(2,1)S(1)} async-done(((bf16[24,4,512]{2,0,1:T(8,128)(2,1)}), bf16[24,4,512]{2,0,1:T(8,128)(2,1)S(1)}, u32[]{:S(2)}, u32[]{:S(2)}) %all-to-all-start.3) | async-done | bytes 98336 | tf_op jit(solution)/shard_map/all_to_all | solution.py:51
  27.3 3.3 %all-to-all-start.5 = ((bf16[24,4,512]{2,0,1:T(8,128)(2,1)}), bf16[24,4,512]{2,0,1:T(8,128)(2,1)S(1)}, u32[]{:S(2)}, u32[]{:S(2)}) async-start(bf16[24,4,512]{2,0,1:T(8,128)(2,1)} %copy.40), calls=%async_computation.5 | async-start | bytes 196608 | tf_op jit(solution)/shard_map/all_to_all | solution.py:50
  31.3 4.2 %all-to-all-done.5 = bf16[24,4,512]{2,0,1:T(8,128)(2,1)S(1)} async-done(((bf16[24,4,512]{2,0,1:T(8,128)(2,1)}), bf16[24,4,512]{2,0,1:T(8,128)(2,1)S(1)}, u32[]{:S(2)}, u32[]{:S(2)}) %all-to-all-start.5) | async-done | bytes 98336 | tf_op jit(solution)/shard_map/all_to_all | solution.py:50
  35.5 3.3 %all-to-all-start.7 = ((bf16[24,4,512]{2,0,1:T(8,128)(2,1)}), bf16[24,4,512]{2,0,1:T(8,128)(2,1)S(1)}, u32[]{:S(2)}, u32[]{:S(2)}) async-start(bf16[24,4,512]{2,0,1:T(8,128)(2,1)} %copy.44), calls=%async_computation.7 | async-start | bytes 196608 | tf_op jit(solution)/shard_map/all_to_all | solution.py:51
  39.9 3.8 %all-to-all-done.7 = bf16[24,4,512]{2,0,1:T(8,128)(2,1)S(1)} async-done(((bf16[24,4,512]{2,0,1:T(8,128)(2,1)}), bf16[24,4,512]{2,0,1:T(8,128)(2,1)S(1)}, u32[]{:S(2)}, u32[]{:S(2)}) %all-to-all-start.7) | async-done | bytes 98336 | tf_op jit(solution)/shard_map/all_to_all | solution.py:51
  43.7 3.5 %all-to-all-start = ((bf16[128,4,512]{0,2,1:T(8,128)(2,1)}), bf16[128,4,512]{0,2,1:T(8,128)(2,1)S(1)}, u32[]{:S(2)}, u32[]{:S(2)}) async-start(bf16[128,4,512]{0,2,1:T(8,128)(2,1)} %bitcast.1), calls=%async_computation | async-start | bytes 1048576 | tf_op jit(solution)/shard_map/all_to_all | solution.py:48
  48.3 5.4 %all-to-all-done = bf16[128,4,512]{0,2,1:T(8,128)(2,1)S(1)} async-done(((bf16[128,4,512]{0,2,1:T(8,128)(2,1)}), bf16[128,4,512]{0,2,1:T(8,128)(2,1)S(1)}, u32[]{:S(2)}, u32[]{:S(2)}) %all-to-all-start) | async-done | bytes 524320 | tf_op jit(solution)/shard_map/all_to_all | solution.py:48
  53.7 3.5 %all-to-all-start.2 = ((bf16[128,4,512]{0,2,1:T(8,128)(2,1)}), bf16[128,4,512]{0,2,1:T(8,128)(2,1)S(1)}, u32[]{:S(2)}, u32[]{:S(2)}) async-start(bf16[128,4,512]{0,2,1:T(8,128)(2,1)} %bitcast.4), calls=%async_computation.2 | async-start | bytes 1048576 | tf_op jit(solution)/shard_map/all_to_all | solution.py:49
  57.2 1.0 copy.38
  58.2 6.5 %all-to-all-done.2 = bf16[128,4,512]{0,2,1:T(8,128)(2,1)S(1)} async-done(((bf16[128,4,512]{0,2,1:T(8,128)(2,1)}), bf16[128,4,512]{0,2,1:T(8,128)(2,1)S(1)}, u32[]{:S(2)}, u32[]{:S(2)}) %all-to-all-start.2) | async-done | bytes 524320 | tf_op jit(solution)/shard_map/all_to_all | solution.py:49
  64.8 3.5 %all-to-all-start.4 = ((bf16[128,4,512]{0,2,1:T(8,128)(2,1)}), bf16[128,4,512]{0,2,1:T(8,128)(2,1)S(1)}, u32[]{:S(2)}, u32[]{:S(2)}) async-start(bf16[128,4,512]{0,2,1:T(8,128)(2,1)} %bitcast.13), calls=%async_computation.4 | async-start | bytes 1048576 | tf_op jit(solution)/shard_map/all_to_all | solution.py:48
  72.3 1.0 reshape.99
  73.9 3.1 %all-to-all-done.4 = bf16[128,4,512]{0,2,1:T(8,128)(2,1)S(1)} async-done(((bf16[128,4,512]{0,2,1:T(8,128)(2,1)}), bf16[128,4,512]{0,2,1:T(8,128)(2,1)S(1)}, u32[]{:S(2)}, u32[]{:S(2)}) %all-to-all-start.4) | async-done | bytes 524320 | tf_op jit(solution)/shard_map/all_to_all | solution.py:48
  77.0 3.5 %all-to-all-start.6 = ((bf16[128,4,512]{0,2,1:T(8,128)(2,1)}), bf16[128,4,512]{0,2,1:T(8,128)(2,1)S(1)}, u32[]{:S(2)}, u32[]{:S(2)}) async-start(bf16[128,4,512]{0,2,1:T(8,128)(2,1)} %bitcast.16), calls=%async_computation.6 | async-start | bytes 1048576 | tf_op jit(solution)/shard_map/all_to_all | solution.py:49
  80.7 2.1 %convolution_convert_fusion.2 = bf16[8,96,64]{1,2,0:T(8,128)(2,1)} fusion(bf16[512,8,64]{0,2,1:T(8,128)(2,1)} %reshape.99, f32[8,512,96]{1,2,0:T(8,128)S(1)} %get-tuple-element.13, f32[8,512]{1,0:T(8,128)S(1)} %get-tuple-element.12), kind=kOutput, calls=%fused_computation.24 | convolution fusion | flops 51167232 | bytes 2211840 | tf_op jit(solution)/shard_map/hqk,qhd->khd/dot_general | solution.py:26
  83.9 2.9 %multiply_reduce_fusion.1 = (f32[8,512]{1,0:T(8,128)S(1)}, f32[8,512,96]{1,2,0:T(8,128)}) fusion(f32[8,512,96]{1,2,0:T(8,128)} %copy-done.1, f32[8,512]{1,0:T(8,128)S(1)} %get-tuple-element.12, bf16[512,8,64]{0,2,1:T(8,128)(2,1)S(1)} %copy-done.5, bf16[96,8,64]{2,1,0:T(8,128)(2,1)S(1)} %copy-done.11), kind=kOutput, calls=%fused_computation.19 | convolution fusion | flops 51507200 | bytes 3801088 | tf_op jit(solution)/shard_map/qhd,khd->hqk/dot_general | solution.py:21
  89.7 1.3 copy-done.2
  91.4 1.3 slice-done.3
  92.7 1.4 fusion.5
  95.3 1.4 convolution_add_fusion.2
  96.7 1.4 convolution_add_fusion.1
  98.1 2.6 %convolution_add_fusion = f32[96,4096]{1,0:T(8,128)} fusion(f32[96,4096]{1,0:T(8,128)S(1)} %convolution_add_fusion.1, bf16[96,512]{0,1:T(8,128)(2,1)S(1)} %bitcast.86, bf16[2,4096,512]{2,1,0:T(8,128)(2,1)S(1)} %bitcast.74), kind=kOutput, calls=%fused_computation.2 | convolution fusion | flops 403046400 | bytes 7471104 | tf_op jit(solution)/shard_map/rc,dc->rd/dot_general | solution.py:64
  102.7 30.5 %reduce-scatter.4.cloned.1.call-done = f32[24,4096]{1,0:T(8,128)} async-done(((f32[96,4096]{1,0:T(8,128)}), f32[24,4096]{1,0:T(8,128)}) %reduce-scatter.4.cloned.1.call-update) | async-done | bytes 393232
  133.3 1.3 fusion.26
  134.5 15.1 %all-reduce.1 = f32[4096]{0:T(1024)S(1)} all-reduce(f32[4096]{0:T(1024)S(1)} %get-tuple-element.2), channel_id=3, replica_groups=mesh['dp'=8,'seq'=4] {'seq'}, use_global_device_ids=true, to_apply=%region_10.0.clone | all-reduce | flops 4096 | bytes 32768
  149.6 13.6 %psum.7 = f32[1024]{0:T(1024)S(1)} all-reduce(f32[1024]{0:T(1024)S(1)} %dynamic-slice.3), channel_id=1, replica_groups=mesh['dp'=8,'seq'=4] {'dp'}, use_global_device_ids=true, to_apply=%region_11.0 | all-reduce | flops 1024 | bytes 8192 | tf_op jit(solution)/shard_map/psum | solution.py:75
  163.3 8.1 %all_gather.3 = f32[4096]{0:T(1024)S(1)} all-gather(f32[1024]{0:T(1024)S(1)} %psum.7), channel_id=1, replica_groups=mesh['dp'=8,'seq'=4] {'seq'}, dimensions={0}, use_global_device_ids=true | all-gather | bytes 20480 | tf_op jit(solution)/shard_map/all_gather | solution.py:76
  172.0 1.8 %fusion.28 = bf16[1,24,4096]{2,1,0:T(8,128)(2,1)} fusion(f32[24,4096]{1,0:T(8,128)} %reduce-scatter.4.cloned.1.call-done, bf16[1,24,4096]{2,1,0:T(8,128)(2,1)S(1)} %copy-done, f32[24]{0:T(128)S(1)} %broadcast_multiply_fusion.1, f32[4096]{0:T(1024)S(1)} %copy-done.13, f32[24]{0:T(128)S(1)} %add_rsqrt_fusion), kind=kLoop, calls=%fused_computation.43 | loop fusion | flops 688128 | bytes 803008 | tf_op jit(solution)/shard_map/broadcast_in_dim | solution.py:78
  (80 shorter events, 18.3 us)
Async XLA Ops:
  7.2 31.6 %copy-start.3 = (bf16[2,1,128,2048]{3,2,1,0:T(8,128)(2,1)S(1)}, bf16[2,1,128,2048]{3,2,1,0:T(8,128)(2,1)}, u32[]{:S(2)}) copy-start(bf16[2,1,128,2048]{3,2,1,0:T(8,128)(2,1)} %param.10) | copy-start | bytes 3145732
  8.9 10.1 %all-to-all-start.1 = ((bf16[24,4,512]{2,0,1:T(8,128)(2,1)}), bf16[24,4,512]{2,0,1:T(8,128)(2,1)S(1)}, u32[]{:S(2)}, u32[]{:S(2)}) async-start(bf16[24,4,512]{2,0,1:T(8,128)(2,1)} %copy.32), calls=%async_computation.1 | async-start | bytes 196608 | tf_op jit(solution)/shard_map/all_to_all | solution.py:50
  19.1 8.2 %all-to-all-start.3 = ((bf16[24,4,512]{2,0,1:T(8,128)(2,1)}), bf16[24,4,512]{2,0,1:T(8,128)(2,1)S(1)}, u32[]{:S(2)}, u32[]{:S(2)}) async-start(bf16[24,4,512]{2,0,1:T(8,128)(2,1)} %copy.36), calls=%async_computation.3 | async-start | bytes 196608 | tf_op jit(solution)/shard_map/all_to_all | solution.py:51
  27.3 8.2 %all-to-all-start.5 = ((bf16[24,4,512]{2,0,1:T(8,128)(2,1)}), bf16[24,4,512]{2,0,1:T(8,128)(2,1)S(1)}, u32[]{:S(2)}, u32[]{:S(2)}) async-start(bf16[24,4,512]{2,0,1:T(8,128)(2,1)} %copy.40), calls=%async_computation.5 | async-start | bytes 196608 | tf_op jit(solution)/shard_map/all_to_all | solution.py:50
  35.5 3.3 %copy-start.6 = (bf16[24,4,512]{2,0,1:T(8,128)(2,1)}, bf16[24,4,512]{2,0,1:T(8,128)(2,1)S(1)}, u32[]{:S(2)}) copy-start(bf16[24,4,512]{2,0,1:T(8,128)(2,1)S(1)} %all-to-all-done.5) | copy-start | bytes 294916
  35.5 8.2 %all-to-all-start.7 = ((bf16[24,4,512]{2,0,1:T(8,128)(2,1)}), bf16[24,4,512]{2,0,1:T(8,128)(2,1)S(1)}, u32[]{:S(2)}, u32[]{:S(2)}) async-start(bf16[24,4,512]{2,0,1:T(8,128)(2,1)} %copy.44), calls=%async_computation.7 | async-start | bytes 196608 | tf_op jit(solution)/shard_map/all_to_all | solution.py:51
  38.9 8.3 %copy-start.4 = (bf16[2,1,128,2048]{3,2,1,0:T(8,128)(2,1)S(1)}, bf16[2,1,128,2048]{3,2,1,0:T(8,128)(2,1)}, u32[]{:S(2)}) copy-start(bf16[2,1,128,2048]{3,2,1,0:T(8,128)(2,1)} %param.11) | copy-start | bytes 3145732
  43.7 3.6 %copy-start.8 = (bf16[24,4,512]{2,0,1:T(8,128)(2,1)}, bf16[24,4,512]{2,0,1:T(8,128)(2,1)S(1)}, u32[]{:S(2)}) copy-start(bf16[24,4,512]{2,0,1:T(8,128)(2,1)S(1)} %all-to-all-done.7) | copy-start | bytes 294916
  43.7 10.0 %all-to-all-start = ((bf16[128,4,512]{0,2,1:T(8,128)(2,1)}), bf16[128,4,512]{0,2,1:T(8,128)(2,1)S(1)}, u32[]{:S(2)}, u32[]{:S(2)}) async-start(bf16[128,4,512]{0,2,1:T(8,128)(2,1)} %bitcast.1), calls=%async_computation | async-start | bytes 1048576 | tf_op jit(solution)/shard_map/all_to_all | solution.py:48
  53.7 11.0 %all-to-all-start.2 = ((bf16[128,4,512]{0,2,1:T(8,128)(2,1)}), bf16[128,4,512]{0,2,1:T(8,128)(2,1)S(1)}, u32[]{:S(2)}, u32[]{:S(2)}) async-start(bf16[128,4,512]{0,2,1:T(8,128)(2,1)} %bitcast.4), calls=%async_computation.2 | async-start | bytes 1048576 | tf_op jit(solution)/shard_map/all_to_all | solution.py:49
  58.2 12.0 %copy-start.7 = (bf16[24,4,512]{2,0,1:T(8,128)(2,1)S(1)}, bf16[24,4,512]{2,0,1:T(8,128)(2,1)}, u32[]{:S(2)}) copy-start(bf16[24,4,512]{2,0,1:T(8,128)(2,1)} %copy-done.6) | copy-start | bytes 294916
  58.2 12.2 %copy-start.9 = (bf16[24,4,512]{2,0,1:T(8,128)(2,1)S(1)}, bf16[24,4,512]{2,0,1:T(8,128)(2,1)}, u32[]{:S(2)}) copy-start(bf16[24,4,512]{2,0,1:T(8,128)(2,1)} %copy-done.8) | copy-start | bytes 294916
  64.8 12.2 %all-to-all-start.4 = ((bf16[128,4,512]{0,2,1:T(8,128)(2,1)}), bf16[128,4,512]{0,2,1:T(8,128)(2,1)S(1)}, u32[]{:S(2)}, u32[]{:S(2)}) async-start(bf16[128,4,512]{0,2,1:T(8,128)(2,1)} %bitcast.13), calls=%async_computation.4 | async-start | bytes 1048576 | tf_op jit(solution)/shard_map/all_to_all | solution.py:48
  73.9 8.9 %copy-start.1 = (f32[8,512,96]{1,2,0:T(8,128)}, f32[8,512,96]{1,2,0:T(8,128)S(1)}, u32[]{:S(2)}) copy-start(f32[8,512,96]{1,2,0:T(8,128)S(1)} %get-tuple-element.13) | copy-start | bytes 4718596
  77.0 10.0 %all-to-all-start.6 = ((bf16[128,4,512]{0,2,1:T(8,128)(2,1)}), bf16[128,4,512]{0,2,1:T(8,128)(2,1)S(1)}, u32[]{:S(2)}, u32[]{:S(2)}) async-start(bf16[128,4,512]{0,2,1:T(8,128)(2,1)} %bitcast.16), calls=%async_computation.6 | async-start | bytes 1048576 | tf_op jit(solution)/shard_map/all_to_all | solution.py:49
  80.4 52.8 %reduce-scatter.4.cloned.1.call-start = ((), (), s32[]{:S(2)}) async-start(), calls=%async_computation.9 | async-start | bytes 1966080
  82.8 1.0 copy-start.5
  82.8 1.1 copy-start.11
  88.2 0.9 copy-start.10
  88.2 1.5 copy-start.15
  88.2 3.2 %slice-start.2 = ((s8[8388608]{0:T(1024)(128)(4,1)}), s8[4194304]{0:T(1024)(128)(4,1)S(1)}, s32[]{:S(2)}) async-start(s8[8388608]{0:T(1024)(128)(4,1)} %bitcast.75), calls=%async_computation.12 | async-start | bytes 8388608
  89.1 1.9 %copy-start.2 = (f32[8,512,96]{1,2,0:T(8,128)S(1)}, f32[8,512,96]{1,2,0:T(8,128)}, u32[]{:S(2)}) copy-start(f32[8,512,96]{1,2,0:T(8,128)} %copy-done.1) | copy-start | bytes 4718596
  89.1 3.6 %slice-start.3 = ((s8[8388608]{0:T(1024)(128)(4,1)}), s8[4194304]{0:T(1024)(128)(4,1)S(1)}, s32[]{:S(2)}) async-start(s8[8388608]{0:T(1024)(128)(4,1)} %bitcast.75), calls=%async_computation.13 | async-start | bytes 8388608
  91.0 3.6 %slice-start = ((s8[8388608]{0:T(1024)(128)(4,1)}), s8[4194304]{0:T(1024)(128)(4,1)S(1)}, s32[]{:S(2)}) async-start(s8[8388608]{0:T(1024)(128)(4,1)} %bitcast.73), calls=%async_computation.10 | async-start | bytes 8388608
  92.7 2.5 %slice-start.1 = ((s8[8388608]{0:T(1024)(128)(4,1)}), s8[4194304]{0:T(1024)(128)(4,1)S(1)}, s32[]{:S(2)}) async-start(s8[8388608]{0:T(1024)(128)(4,1)} %bitcast.73), calls=%async_computation.11 | async-start | bytes 8388608
  94.1 1.1 copy-start.12
  100.7 0.7 copy-start.14
  100.7 1.9 %copy-start = (bf16[1,24,4096]{2,1,0:T(8,128)(2,1)S(1)}, bf16[1,24,4096]{2,1,0:T(8,128)(2,1)}, u32[]{:S(2)}) copy-start(bf16[1,24,4096]{2,1,0:T(8,128)(2,1)} %param.8) | copy-start | bytes 589828
  100.7 32.6 %copy-start.13 = (f32[4096]{0:T(1024)S(1)}, f32[4096]{0:T(1024)}, u32[]{:S(2)}) copy-start(f32[4096]{0:T(1024)} %param.9) | copy-start | bytes 49156
Sparse Core Ops, SparseCore 0:
  100.8 32.3 reduce-scatter.3
where the time goes:
time: 182 us; the launch traced here: 181 us
  waiting for transfers between devices  61.1 us (34%)
  blocking collectives  36.8 us (20%)
  starting transfers between devices  29.2 us (16%)
  local copies, waits for them, and re-layouts  20 us (11%)
  between operations  15 us (8%)
  matrix products  14.6 us (8%)
  other arithmetic  3.87 us (2%)
    unnamed x2, waiting for transfers between devices  30.5 us
    unnamed x1, blocking collectives  15.1 us
    psum x1, blocking collectives, body(): gain_piece = lax.psum(gain_piece, 'dp')  13.6 us
    all_to_all x2, waiting for transfers between devices, body(): lax.all_to_all(query_rows, 'seq', split_axis=1, concat_axis=0, tiled=True)  8.5 us
    all_to_all x2, starting transfers between devices, body(): lax.all_to_all(key_rows, 'seq', split_axis=1, concat_axis=0, tiled=True)  8.5 us
    all_gather x1, blocking collectives, body(): gain_total = lax.all_gather(gain_piece, 'seq', axis=0, tiled=True)  8.08 us
    all_to_all x2, waiting for transfers between devices, body(): lax.all_to_all(value_rows, 'seq', split_axis=1, concat_axis=0, tiled=True)  7.94 us
    all_to_all x2, waiting for transfers between devices, body(): lax.all_to_all(key_rows, 'seq', split_axis=1, concat_axis=0, tiled=True)  7.45 us
  transfers between devices with their start and end apart: 9, of which 9 were waited for; matrix products, arithmetic and copies ran while one was open for 10% of the time, Pallas kernels for 0%

commit v1 on v0

--- a/solution.py
+++ b/solution.py
@@ -2,6 +2,7 @@
 import jax.numpy as jnp
 from jax import lax
 from jax.sharding import PartitionSpec as P
+from jax.lax import ppermute, psum
 
 HEAD_DIM = 64
 
@@ -72,7 +73,20 @@
     grad_rows_out = inv_rms * (scaled - normed * jnp.mean(scaled * normed, axis=-1, keepdims=True))
     gain_term = jnp.sum(state_grad * normed, axis=0)
     gain_piece = lax.psum_scatter(gain_term, "seq", scatter_dimension=0, tiled=True)
-    gain_piece = lax.psum(gain_piece, "dp")
+
+    def pairs_all_produce(chunk):
+        dev_count = psum(1, axis_name="dp")
+        kept_arr, val2 = (chunk, 0)
+        while 1 << val2 < dev_count:
+            vals = []
+            for t in range(dev_count):
+                vals.append((t, t ^ 1 << val2))
+            block_out = ppermute(kept_arr, axis_name="dp", perm=vals)
+            kept_arr = kept_arr + block_out
+            val2 = val2 + 1
+        return kept_arr
+
+    gain_piece = pairs_all_produce(gain_piece)
     gain_total = lax.all_gather(gain_piece, "seq", axis=0, tiled=True)
     gain_grad = gain_total / lax.axis_size("dp")
     return (grad_rows_out.astype(jnp.bfloat16)[None], gain_grad)

time: 182 us -> 175 us (0.962)
  blocking collectives: 36.8 us -> 23.2 us
  starting transfers between devices: 29.2 us -> 33.1 us
  waiting for transfers between devices: 61.1 us -> 64.8 us
    psum x1 -> x0, blocking collectives: 13.6 us -> none  [body(): gain_piece = lax.psum(gain_piece, 'dp')]
    ppermute x0 -> x3, starting transfers between devices: none -> 3.9 us  [pairs_all_produce(): block_out = ppermute(kept_arr, axis_name='dp', perm=vals)]
    ppermute x0 -> x3, waiting for transfers between devices: none -> 3.56 us  [pairs_all_produce(): block_out = ppermute(kept_arr, axis_name='dp', perm=vals)]
  transfers between devices with their start and end apart: 9 -> 12, of which waited for: 9 -> 12; matrix products, arithmetic and copies ran while one was open for 10% -> 11% of each run, Pallas kernels for 0% -> 0%
where the time goes in v1:
time: 175 us; the launch traced here: 174 us
  waiting for transfers between devices  64.8 us (37%)
  starting transfers between devices  33.1 us (19%)
  blocking collectives  23.2 us (13%)
  local copies, waits for them, and re-layouts  20 us (11%)
  between operations  15 us (9%)
  matrix products  14.5 us (8%)
  other arithmetic  3.88 us (2%)
    unnamed x2, waiting for transfers between devices  30.5 us
    unnamed x1, blocking collectives  15.1 us
    all_to_all x2, waiting for transfers between devices, body(): lax.all_to_all(query_rows, 'seq', split_axis=1, concat_axis=0, tiled=True)  8.55 us
    all_to_all x2, starting transfers between devices, body(): lax.all_to_all(key_rows, 'seq', split_axis=1, concat_axis=0, tiled=True)  8.5 us
    all_gather x1, blocking collectives, body(): gain_total = lax.all_gather(gain_piece, 'seq', axis=0, tiled=True)  8.07 us
    all_to_all x2, waiting for transfers between devices, body(): lax.all_to_all(value_rows, 'seq', split_axis=1, concat_axis=0, tiled=True)  7.93 us
    all_to_all x2, waiting for transfers between devices, body(): lax.all_to_all(key_rows, 'seq', split_axis=1, concat_axis=0, tiled=True)  7.45 us
    all_to_all x2, starting transfers between devices, body(): lax.all_to_all(query_rows, 'seq', split_axis=1, concat_axis=0, tiled=True)  6.94 us
  transfers between devices with their start and end apart: 12, of which 12 were waited for; matrix products, arithmetic and copies ran while one was open for 11% of the time, Pallas kernels for 0%

profile of v1, /device:TPU:0, one launch (start us, length us, event | category | flops | bytes accessed | tf_op | source)
XLA Modules:
  0.0 174.4 jit_solution(10650280582918020598)
XLA Ops:
  8.9 5.2 %all-to-all-start.1 = ((bf16[24,4,512]{2,0,1:T(8,128)(2,1)}), bf16[24,4,512]{2,0,1:T(8,128)(2,1)S(1)}, u32[]{:S(2)}, u32[]{:S(2)}) async-start(bf16[24,4,512]{2,0,1:T(8,128)(2,1)} %copy.32), calls=%async_computation.1 | async-start | bytes 196608 | tf_op jit(solution)/shard_map/all_to_all | solution.py:51
  15.8 3.3 %all-to-all-done.1 = bf16[24,4,512]{2,0,1:T(8,128)(2,1)S(1)} async-done(((bf16[24,4,512]{2,0,1:T(8,128)(2,1)}), bf16[24,4,512]{2,0,1:T(8,128)(2,1)S(1)}, u32[]{:S(2)}, u32[]{:S(2)}) %all-to-all-start.1) | async-done | bytes 98336 | tf_op jit(solution)/shard_map/all_to_all | solution.py:51
  19.1 3.3 %all-to-all-start.3 = ((bf16[24,4,512]{2,0,1:T(8,128)(2,1)}), bf16[24,4,512]{2,0,1:T(8,128)(2,1)S(1)}, u32[]{:S(2)}, u32[]{:S(2)}) async-start(bf16[24,4,512]{2,0,1:T(8,128)(2,1)} %copy.36), calls=%async_computation.3 | async-start | bytes 196608 | tf_op jit(solution)/shard_map/all_to_all | solution.py:52
  23.1 4.2 %all-to-all-done.3 = bf16[24,4,512]{2,0,1:T(8,128)(2,1)S(1)} async-done(((bf16[24,4,512]{2,0,1:T(8,128)(2,1)}), bf16[24,4,512]{2,0,1:T(8,128)(2,1)S(1)}, u32[]{:S(2)}, u32[]{:S(2)}) %all-to-all-start.3) | async-done | bytes 98336 | tf_op jit(solution)/shard_map/all_to_all | solution.py:52
  27.3 3.3 %all-to-all-start.5 = ((bf16[24,4,512]{2,0,1:T(8,128)(2,1)}), bf16[24,4,512]{2,0,1:T(8,128)(2,1)S(1)}, u32[]{:S(2)}, u32[]{:S(2)}) async-start(bf16[24,4,512]{2,0,1:T(8,128)(2,1)} %copy.40), calls=%async_computation.5 | async-start | bytes 196608 | tf_op jit(solution)/shard_map/all_to_all | solution.py:51
  31.3 4.2 %all-to-all-done.5 = bf16[24,4,512]{2,0,1:T(8,128)(2,1)S(1)} async-done(((bf16[24,4,512]{2,0,1:T(8,128)(2,1)}), bf16[24,4,512]{2,0,1:T(8,128)(2,1)S(1)}, u32[]{:S(2)}, u32[]{:S(2)}) %all-to-all-start.5) | async-done | bytes 98336 | tf_op jit(solution)/shard_map/all_to_all | solution.py:51
  35.5 3.3 %all-to-all-start.7 = ((bf16[24,4,512]{2,0,1:T(8,128)(2,1)}), bf16[24,4,512]{2,0,1:T(8,128)(2,1)S(1)}, u32[]{:S(2)}, u32[]{:S(2)}) async-start(bf16[24,4,512]{2,0,1:T(8,128)(2,1)} %copy.44), calls=%async_computation.7 | async-start | bytes 196608 | tf_op jit(solution)/shard_map/all_to_all | solution.py:52
  40.0 3.7 %all-to-all-done.7 = bf16[24,4,512]{2,0,1:T(8,128)(2,1)S(1)} async-done(((bf16[24,4,512]{2,0,1:T(8,128)(2,1)}), bf16[24,4,512]{2,0,1:T(8,128)(2,1)S(1)}, u32[]{:S(2)}, u32[]{:S(2)}) %all-to-all-start.7) | async-done | bytes 98336 | tf_op jit(solution)/shard_map/all_to_all | solution.py:52
  43.7 3.5 %all-to-all-start = ((bf16[128,4,512]{0,2,1:T(8,128)(2,1)}), bf16[128,4,512]{0,2,1:T(8,128)(2,1)S(1)}, u32[]{:S(2)}, u32[]{:S(2)}) async-start(bf16[128,4,512]{0,2,1:T(8,128)(2,1)} %bitcast.1), calls=%async_computation | async-start | bytes 1048576 | tf_op jit(solution)/shard_map/all_to_all | solution.py:49
  48.3 5.4 %all-to-all-done = bf16[128,4,512]{0,2,1:T(8,128)(2,1)S(1)} async-done(((bf16[128,4,512]{0,2,1:T(8,128)(2,1)}), bf16[128,4,512]{0,2,1:T(8,128)(2,1)S(1)}, u32[]{:S(2)}, u32[]{:S(2)}) %all-to-all-start) | async-done | bytes 524320 | tf_op jit(solution)/shard_map/all_to_all | solution.py:49
  53.7 3.5 %all-to-all-start.2 = ((bf16[128,4,512]{0,2,1:T(8,128)(2,1)}), bf16[128,4,512]{0,2,1:T(8,128)(2,1)S(1)}, u32[]{:S(2)}, u32[]{:S(2)}) async-start(bf16[128,4,512]{0,2,1:T(8,128)(2,1)} %bitcast.4), calls=%async_computation.2 | async-start | bytes 1048576 | tf_op jit(solution)/shard_map/all_to_all | solution.py:50
  58.2 6.5 %all-to-all-done.2 = bf16[128,4,512]{0,2,1:T(8,128)(2,1)S(1)} async-done(((bf16[128,4,512]{0,2,1:T(8,128)(2,1)}), bf16[128,4,512]{0,2,1:T(8,128)(2,1)S(1)}, u32[]{:S(2)}, u32[]{:S(2)}) %all-to-all-start.2) | async-done | bytes 524320 | tf_op jit(solution)/shard_map/all_to_all | solution.py:50
  64.8 3.5 %all-to-all-start.4 = ((bf16[128,4,512]{0,2,1:T(8,128)(2,1)}), bf16[128,4,512]{0,2,1:T(8,128)(2,1)S(1)}, u32[]{:S(2)}, u32[]{:S(2)}) async-start(bf16[128,4,512]{0,2,1:T(8,128)(2,1)} %bitcast.13), calls=%async_computation.4 | async-start | bytes 1048576 | tf_op jit(solution)/shard_map/all_to_all | solution.py:49
  73.8 3.1 %all-to-all-done.4 = bf16[128,4,512]{0,2,1:T(8,128)(2,1)S(1)} async-done(((bf16[128,4,512]{0,2,1:T(8,128)(2,1)}), bf16[128,4,512]{0,2,1:T(8,128)(2,1)S(1)}, u32[]{:S(2)}, u32[]{:S(2)}) %all-to-all-start.4) | async-done | bytes 524320 | tf_op jit(solution)/shard_map/all_to_all | solution.py:49
  77.0 3.5 %all-to-all-start.6 = ((bf16[128,4,512]{0,2,1:T(8,128)(2,1)}), bf16[128,4,512]{0,2,1:T(8,128)(2,1)S(1)}, u32[]{:S(2)}, u32[]{:S(2)}) async-start(bf16[128,4,512]{0,2,1:T(8,128)(2,1)} %bitcast.16), calls=%async_computation.6 | async-start | bytes 1048576 | tf_op jit(solution)/shard_map/all_to_all | solution.py:50
  80.7 2.1 %convolution_convert_fusion.2 = bf16[8,96,64]{1,2,0:T(8,128)(2,1)} fusion(bf16[512,8,64]{0,2,1:T(8,128)(2,1)} %reshape.99, f32[8,512,96]{1,2,0:T(8,128)S(1)} %get-tuple-element.13, f32[8,512]{1,0:T(8,128)S(1)} %get-tuple-element.12), kind=kOutput, calls=%fused_computation.24 | convolution fusion | flops 51167232 | bytes 2211840 | tf_op jit(solution)/shard_map/hqk,qhd->khd/dot_general | solution.py:27
  83.9 2.9 %multiply_reduce_fusion.1 = (f32[8,512]{1,0:T(8,128)S(1)}, f32[8,512,96]{1,2,0:T(8,128)}) fusion(f32[8,512,96]{1,2,0:T(8,128)} %copy-done.1, f32[8,512]{1,0:T(8,128)S(1)} %get-tuple-element.12, bf16[512,8,64]{0,2,1:T(8,128)(2,1)S(1)} %copy-done.5, bf16[96,8,64]{2,1,0:T(8,128)(2,1)S(1)} %copy-done.11), kind=kOutput, calls=%fused_computation.19 | convolution fusion | flops 51507200 | bytes 3801088 | tf_op jit(solution)/shard_map/qhd,khd->hqk/dot_general | solution.py:22
  89.7 1.3 copy-done.2
  91.4 1.3 slice-done.3
  92.7 1.4 fusion.5
  95.3 1.4 convolution_add_fusion.2
  96.7 1.4 convolution_add_fusion.1
  98.1 2.6 %convolution_add_fusion = f32[96,4096]{1,0:T(8,128)} fusion(f32[96,4096]{1,0:T(8,128)S(1)} %convolution_add_fusion.1, bf16[96,512]{0,1:T(8,128)(2,1)S(1)} %bitcast.86, bf16[2,4096,512]{2,1,0:T(8,128)(2,1)S(1)} %bitcast.74), kind=kOutput, calls=%fused_computation.2 | convolution fusion | flops 403046400 | bytes 7471104 | tf_op jit(solution)/shard_map/rc,dc->rd/dot_general | solution.py:65
  102.7 30.5 %reduce-scatter.4.cloned.1.call-done = f32[24,4096]{1,0:T(8,128)} async-done(((f32[96,4096]{1,0:T(8,128)}), f32[24,4096]{1,0:T(8,128)}) %reduce-scatter.4.cloned.1.call-update) | async-done | bytes 393232
  133.2 1.3 fusion.26
  134.5 15.1 %all-reduce.1 = f32[4096]{0:T(1024)S(1)} all-reduce(f32[4096]{0:T(1024)S(1)} %get-tuple-element.2), channel_id=3, replica_groups=mesh['dp'=8,'seq'=4] {'seq'}, use_global_device_ids=true, to_apply=%region_10.0.clone | all-reduce | flops 4096 | bytes 32768
  149.6 1.2 collective-permute-done
  150.8 1.5 collective-permute-start.1
  152.3 2.1 %collective-permute-done.1 = f32[1024]{0:T(1024)S(1)} collective-permute-done((f32[1024]{0:T(1024)S(1)}, f32[1024]{0:T(1024)S(1)}, u32[]{:S(2)}, u32[]{:S(2)}) %collective-permute-start.1) | collective-permute-done | bytes 4128 | tf_op jit(solution)/shard_map/ppermute | solution.py:84
  154.4 2.4 %collective-permute-start.2 = (f32[1024]{0:T(1024)S(1)}, f32[1024]{0:T(1024)S(1)}, u32[]{:S(2)}, u32[]{:S(2)}) collective-permute-start(f32[1024]{0:T(1024)S(1)} %add.35), channel_id=1, source_target_pairs={{0,16},{4,20},{8,24},{12,28},{16,0},{20,4},{24,8},{28,12},{1,17},{... | collective-permute-start | bytes 12296 | tf_op jit(solution)/shard_map/ppermute | solution.py:84
  156.8 1.8 %fusion.28 = bf16[1,24,4096]{2,1,0:T(8,128)(2,1)} fusion(f32[24,4096]{1,0:T(8,128)} %reduce-scatter.4.cloned.1.call-done, bf16[1,24,4096]{2,1,0:T(8,128)(2,1)S(1)} %copy-done, f32[24]{0:T(128)S(1)} %broadcast_multiply_fusion.1, f32[4096]{0:T(1024)S(1)} %copy-done.13, f32[24]{0:T(128)S(1)} %add_rsqrt_fusion), kind=kLoop, calls=%fused_computation.43 | loop fusion | flops 688128 | bytes 803008 | tf_op jit(solution)/shard_map/broadcast_in_dim | solution.py:92
  158.9 8.1 %all_gather.3 = f32[4096]{0:T(1024)S(1)} all-gather(f32[1024]{0:T(1024)S(1)} %add.36), channel_id=1, replica_groups=mesh['dp'=8,'seq'=4] {'seq'}, dimensions={0}, use_global_device_ids=true | all-gather | bytes 20480 | tf_op jit(solution)/shard_map/all_gather | solution.py:90
  (88 shorter events, 21.7 us)
Async XLA Ops:
  7.2 31.6 %copy-start.3 = (bf16[2,1,128,2048]{3,2,1,0:T(8,128)(2,1)S(1)}, bf16[2,1,128,2048]{3,2,1,0:T(8,128)(2,1)}, u32[]{:S(2)}) copy-start(bf16[2,1,128,2048]{3,2,1,0:T(8,128)(2,1)} %param.10) | copy-start | bytes 3145732
  8.9 10.1 %all-to-all-start.1 = ((bf16[24,4,512]{2,0,1:T(8,128)(2,1)}), bf16[24,4,512]{2,0,1:T(8,128)(2,1)S(1)}, u32[]{:S(2)}, u32[]{:S(2)}) async-start(bf16[24,4,512]{2,0,1:T(8,128)(2,1)} %copy.32), calls=%async_computation.1 | async-start | bytes 196608 | tf_op jit(solution)/shard_map/all_to_all | solution.py:51
  19.1 8.2 %all-to-all-start.3 = ((bf16[24,4,512]{2,0,1:T(8,128)(2,1)}), bf16[24,4,512]{2,0,1:T(8,128)(2,1)S(1)}, u32[]{:S(2)}, u32[]{:S(2)}) async-start(bf16[24,4,512]{2,0,1:T(8,128)(2,1)} %copy.36), calls=%async_computation.3 | async-start | bytes 196608 | tf_op jit(solution)/shard_map/all_to_all | solution.py:52
  27.3 8.2 %all-to-all-start.5 = ((bf16[24,4,512]{2,0,1:T(8,128)(2,1)}), bf16[24,4,512]{2,0,1:T(8,128)(2,1)S(1)}, u32[]{:S(2)}, u32[]{:S(2)}) async-start(bf16[24,4,512]{2,0,1:T(8,128)(2,1)} %copy.40), calls=%async_computation.5 | async-start | bytes 196608 | tf_op jit(solution)/shard_map/all_to_all | solution.py:51
  35.5 3.3 %copy-start.6 = (bf16[24,4,512]{2,0,1:T(8,128)(2,1)}, bf16[24,4,512]{2,0,1:T(8,128)(2,1)S(1)}, u32[]{:S(2)}) copy-start(bf16[24,4,512]{2,0,1:T(8,128)(2,1)S(1)} %all-to-all-done.5) | copy-start | bytes 294916
  35.5 8.2 %all-to-all-start.7 = ((bf16[24,4,512]{2,0,1:T(8,128)(2,1)}), bf16[24,4,512]{2,0,1:T(8,128)(2,1)S(1)}, u32[]{:S(2)}, u32[]{:S(2)}) async-start(bf16[24,4,512]{2,0,1:T(8,128)(2,1)} %copy.44), calls=%async_computation.7 | async-start | bytes 196608 | tf_op jit(solution)/shard_map/all_to_all | solution.py:52
  38.9 8.3 %copy-start.4 = (bf16[2,1,128,2048]{3,2,1,0:T(8,128)(2,1)S(1)}, bf16[2,1,128,2048]{3,2,1,0:T(8,128)(2,1)}, u32[]{:S(2)}) copy-start(bf16[2,1,128,2048]{3,2,1,0:T(8,128)(2,1)} %param.11) | copy-start | bytes 3145732
  43.7 3.6 %copy-start.8 = (bf16[24,4,512]{2,0,1:T(8,128)(2,1)}, bf16[24,4,512]{2,0,1:T(8,128)(2,1)S(1)}, u32[]{:S(2)}) copy-start(bf16[24,4,512]{2,0,1:T(8,128)(2,1)S(1)} %all-to-all-done.7) | copy-start | bytes 294916
  43.7 10.0 %all-to-all-start = ((bf16[128,4,512]{0,2,1:T(8,128)(2,1)}), bf16[128,4,512]{0,2,1:T(8,128)(2,1)S(1)}, u32[]{:S(2)}, u32[]{:S(2)}) async-start(bf16[128,4,512]{0,2,1:T(8,128)(2,1)} %bitcast.1), calls=%async_computation | async-start | bytes 1048576 | tf_op jit(solution)/shard_map/all_to_all | solution.py:49
  53.7 11.0 %all-to-all-start.2 = ((bf16[128,4,512]{0,2,1:T(8,128)(2,1)}), bf16[128,4,512]{0,2,1:T(8,128)(2,1)S(1)}, u32[]{:S(2)}, u32[]{:S(2)}) async-start(bf16[128,4,512]{0,2,1:T(8,128)(2,1)} %bitcast.4), calls=%async_computation.2 | async-start | bytes 1048576 | tf_op jit(solution)/shard_map/all_to_all | solution.py:50
  58.2 12.0 %copy-start.7 = (bf16[24,4,512]{2,0,1:T(8,128)(2,1)S(1)}, bf16[24,4,512]{2,0,1:T(8,128)(2,1)}, u32[]{:S(2)}) copy-start(bf16[24,4,512]{2,0,1:T(8,128)(2,1)} %copy-done.6) | copy-start | bytes 294916
  58.2 12.2 %copy-start.9 = (bf16[24,4,512]{2,0,1:T(8,128)(2,1)S(1)}, bf16[24,4,512]{2,0,1:T(8,128)(2,1)}, u32[]{:S(2)}) copy-start(bf16[24,4,512]{2,0,1:T(8,128)(2,1)} %copy-done.8) | copy-start | bytes 294916
  64.8 12.2 %all-to-all-start.4 = ((bf16[128,4,512]{0,2,1:T(8,128)(2,1)}), bf16[128,4,512]{0,2,1:T(8,128)(2,1)S(1)}, u32[]{:S(2)}, u32[]{:S(2)}) async-start(bf16[128,4,512]{0,2,1:T(8,128)(2,1)} %bitcast.13), calls=%async_computation.4 | async-start | bytes 1048576 | tf_op jit(solution)/shard_map/all_to_all | solution.py:49
  73.8 9.0 %copy-start.1 = (f32[8,512,96]{1,2,0:T(8,128)}, f32[8,512,96]{1,2,0:T(8,128)S(1)}, u32[]{:S(2)}) copy-start(f32[8,512,96]{1,2,0:T(8,128)S(1)} %get-tuple-element.13) | copy-start | bytes 4718596
  77.0 10.0 %all-to-all-start.6 = ((bf16[128,4,512]{0,2,1:T(8,128)(2,1)}), bf16[128,4,512]{0,2,1:T(8,128)(2,1)S(1)}, u32[]{:S(2)}, u32[]{:S(2)}) async-start(bf16[128,4,512]{0,2,1:T(8,128)(2,1)} %bitcast.16), calls=%async_computation.6 | async-start | bytes 1048576 | tf_op jit(solution)/shard_map/all_to_all | solution.py:50
  80.4 52.8 %reduce-scatter.4.cloned.1.call-start = ((), (), s32[]{:S(2)}) async-start(), calls=%async_computation.9 | async-start | bytes 1966080
  82.8 1.0 copy-start.5
  82.8 1.1 copy-start.11
  88.2 0.9 copy-start.10
  88.2 1.5 copy-start.15
  88.2 3.2 %slice-start.2 = ((s8[8388608]{0:T(1024)(128)(4,1)}), s8[4194304]{0:T(1024)(128)(4,1)S(1)}, s32[]{:S(2)}) async-start(s8[8388608]{0:T(1024)(128)(4,1)} %bitcast.75), calls=%async_computation.12 | async-start | bytes 8388608
  89.1 1.9 %copy-start.2 = (f32[8,512,96]{1,2,0:T(8,128)S(1)}, f32[8,512,96]{1,2,0:T(8,128)}, u32[]{:S(2)}) copy-start(f32[8,512,96]{1,2,0:T(8,128)} %copy-done.1) | copy-start | bytes 4718596
  89.1 3.6 %slice-start.3 = ((s8[8388608]{0:T(1024)(128)(4,1)}), s8[4194304]{0:T(1024)(128)(4,1)S(1)}, s32[]{:S(2)}) async-start(s8[8388608]{0:T(1024)(128)(4,1)} %bitcast.75), calls=%async_computation.13 | async-start | bytes 8388608
  91.0 3.6 %slice-start = ((s8[8388608]{0:T(1024)(128)(4,1)}), s8[4194304]{0:T(1024)(128)(4,1)S(1)}, s32[]{:S(2)}) async-start(s8[8388608]{0:T(1024)(128)(4,1)} %bitcast.73), calls=%async_computation.10 | async-start | bytes 8388608
  92.7 2.5 %slice-start.1 = ((s8[8388608]{0:T(1024)(128)(4,1)}), s8[4194304]{0:T(1024)(128)(4,1)S(1)}, s32[]{:S(2)}) async-start(s8[8388608]{0:T(1024)(128)(4,1)} %bitcast.73), calls=%async_computation.11 | async-start | bytes 8388608
  94.1 1.1 copy-start.12
  100.7 0.7 copy-start.14
  100.7 1.9 %copy-start = (bf16[1,24,4096]{2,1,0:T(8,128)(2,1)S(1)}, bf16[1,24,4096]{2,1,0:T(8,128)(2,1)}, u32[]{:S(2)}) copy-start(bf16[1,24,4096]{2,1,0:T(8,128)(2,1)} %param.8) | copy-start | bytes 589828
  100.7 32.6 %copy-start.13 = (f32[4096]{0:T(1024)S(1)}, f32[4096]{0:T(1024)}, u32[]{:S(2)}) copy-start(f32[4096]{0:T(1024)} %param.9) | copy-start | bytes 49156
  149.6 1.2 collective-permute-start
  150.8 3.6 %collective-permute-start.1 = (f32[1024]{0:T(1024)S(1)}, f32[1024]{0:T(1024)S(1)}, u32[]{:S(2)}, u32[]{:S(2)}) collective-permute-start(f32[1024]{0:T(1024)S(1)} %dynamic-slice_add_fusion), channel_id=1, source_target_pairs={{0,8},{4,12},{8,0},{12,4},{16,24},{20,28},{24,16},{28,20},{1,9},{5... | collective-permute-start | bytes 12296 | tf_op jit(solution)/shard_map/ppermute | solution.py:84
  154.4 4.5 %collective-permute-start.2 = (f32[1024]{0:T(1024)S(1)}, f32[1024]{0:T(1024)S(1)}, u32[]{:S(2)}, u32[]{:S(2)}) collective-permute-start(f32[1024]{0:T(1024)S(1)} %add.35), channel_id=1, source_target_pairs={{0,16},{4,20},{8,24},{12,28},{16,0},{20,4},{24,8},{28,12},{1,17},{... | collective-permute-start | bytes 12296 | tf_op jit(solution)/shard_map/ppermute | solution.py:84
Sparse Core Ops, SparseCore 0:
  100.8 32.3 reduce-scatter.3
